TPU v7x, 32 devices: a whole 2x2x4 slice. The times are simulated.
32 devices in a mesh: fsdp: 2 (over core), ctx: 4 (over y, x), tp: 4 (over z).
Axes of the slice: x: 2, y: 2, z: 4, core: 2. Of those that a mesh axis runs over, the one named last changes fastest.
Arguments:
- x_prompt: bfloat16 [2, 1024, 1024], P('fsdp', 'ctx'), may hold values from -6 to 6
- x_cont: bfloat16 [2, 12, 256, 1024], P('fsdp', 'ctx'), may hold values from -6 to 6
- cont_start: int32 [2, 12], P('fsdp', 'ctx'), may hold values from 512 to 1024
- w_qkv: bfloat16 [1024, 3, 1024], P(('fsdp', 'ctx'), None, 'tp'), may hold values from -0.1875 to 0.1875
- qkv_bias: bfloat16 [3, 1024], P(None, 'tp'), may hold values from -3 to 3
- w_dense: bfloat16 [1024, 1024], P('tp', ('fsdp', 'ctx')), may hold values from -0.75 to 0.75
- dense_bias: bfloat16 [1024], P(('fsdp', 'ctx')), may hold values from -3 to 3
- w_fc1: bfloat16 [1024, 4096], P(('fsdp', 'ctx'), 'tp'), may hold values from -0.1875 to 0.1875
- fc1_bias: bfloat16 [4096], P('tp'), may hold values from -3 to 3
- w_fc2: bfloat16 [4096, 1024], P('tp', ('fsdp', 'ctx')), may hold values from -0.09375 to 0.09375
- fc2_bias: bfloat16 [1024], P(('fsdp', 'ctx')), may hold values from -3 to 3
- ln1_gain: bfloat16 [1024], P(('fsdp', 'ctx')), may hold values from 0.099609375 to 1.8984375
- ln1_bias: bfloat16 [1024], P(('fsdp', 'ctx')), may hold values from -2 to 2
- ln2_gain: bfloat16 [1024], P(('fsdp', 'ctx')), may hold values from 0.099609375 to 1.8984375
- ln2_bias: bfloat16 [1024], P(('fsdp', 'ctx')), may hold values from -2 to 2
- dy_prompt: bfloat16 [2, 1024, 1024], P('fsdp', 'ctx'), may hold values from -6 to 6
- dy_cont: bfloat16 [2, 12, 256, 1024], P('fsdp', 'ctx'), may hold values from -6 to 6
Outputs:
- y_prompt: float32 [2, 1024, 1024], P('fsdp', 'ctx')
- y_cont: float32 [2, 12, 256, 1024], P('fsdp', 'ctx')
- dx_prompt: float32 [2, 1024, 1024], P('fsdp', 'ctx')
- dx_cont: float32 [2, 12, 256, 1024], P('fsdp', 'ctx')
- d_w_qkv: float32 [1024, 3, 1024], P(('fsdp', 'ctx'), None, 'tp')
- d_qkv_bias: float32 [3, 1024], P(None, 'tp')
- d_w_dense: float32 [1024, 1024], P('tp', ('fsdp', 'ctx'))
- d_dense_bias: float32 [1024], P(('fsdp', 'ctx'))
- d_w_fc1: float32 [1024, 4096], P(('fsdp', 'ctx'), 'tp')
- d_fc1_bias: float32 [4096], P('tp')
- d_w_fc2: float32 [4096, 1024], P('tp', ('fsdp', 'ctx'))
- d_fc2_bias: float32 [1024], P(('fsdp', 'ctx'))
- d_ln1_gain: float32 [1024], P(('fsdp', 'ctx'))
- d_ln1_bias: float32 [1024], P(('fsdp', 'ctx'))
- d_ln2_gain: float32 [1024], P(('fsdp', 'ctx'))
- d_ln2_bias: float32 [1024], P(('fsdp', 'ctx'))
Inputs may be any that keep to these rules, and one draw needn't show every extreme that they name: `cont_start`: a continuation follows the prompt tokens before its first position.
All inputs are finite; a program needn't handle non-finite values.
Results may differ from a plain program's by a relative error of at most 0.012.
Values may be sent and summed in bfloat16 or wider, within the bound.
A program may use at most 192 MiB of HBM per device.

v0:
```python
import jax
import jax.numpy as jnp
from jax import lax
from jax.sharding import PartitionSpec as P

HD = 64
ROT = 16
EPS = 1e-05


def exact_gelu(values):
    return jax.nn.gelu(values, approximate=False)


def rotary_tables(positions):
    freq_index = jnp.arange(ROT // 2).astype(jnp.float32)
    inverse = jnp.power(10000.0, -2.0 * freq_index / ROT)
    phase = positions.astype(jnp.float32)[..., None] * inverse
    cos_half = jnp.cos(phase)
    sin_half = jnp.sin(phase)
    return (
        jnp.concatenate([cos_half, cos_half], axis=-1),
        jnp.concatenate([sin_half, sin_half], axis=-1),
    )


def rotate(inputs, cos_t, sin_t):
    leading = inputs[..., :ROT]
    half_rot = ROT // 2
    turned = jnp.concatenate([-leading[..., half_rot:], leading[..., :half_rot]], axis=-1)
    return jnp.concatenate([leading * cos_t + turned * sin_t, inputs[..., ROT:]], axis=-1)


def masked_scores(
    queries, all_keys, key_limit, query_slot, query_offs, prompt_len, key_slot, key_offs
):
    raw_scores = jnp.einsum("qhd,khd->hqk", queries, all_keys, preferred_element_type=jnp.float32)
    key_index = jnp.arange(all_keys.shape[0], dtype=jnp.int32)
    near_keys = key_index[None, :] < key_limit[:, None]
    own_keys = (key_slot[None, :] == query_slot[:, None]) & (
        key_offs[None, :] <= query_offs[:, None]
    )
    allowed = jnp.where((key_index < prompt_len)[None, :], near_keys, own_keys)
    return jnp.where(allowed[None], raw_scores * 0.125, -1e30)


def on_device(
    x_prompt,
    x_cont,
    cont_start,
    w_qkv,
    qkv_bias,
    w_dense,
    dense_bias,
    w_fc1,
    fc1_bias,
    w_fc2,
    fc2_bias,
    ln1_gain,
    ln1_bias,
    ln2_gain,
    ln2_bias,
    dy_prompt,
    dy_cont,
):
    gathered = (
        lax.all_gather(w_qkv, ("fsdp", "ctx"), axis=0, tiled=True),
        lax.all_gather(w_dense, ("fsdp", "ctx"), axis=1, tiled=True),
        lax.all_gather(w_fc1, ("fsdp", "ctx"), axis=0, tiled=True),
        lax.all_gather(w_fc2, ("fsdp", "ctx"), axis=1, tiled=True),
        lax.all_gather(dense_bias, ("fsdp", "ctx"), axis=0, tiled=True),
        lax.all_gather(fc2_bias, ("fsdp", "ctx"), axis=0, tiled=True),
        lax.all_gather(ln1_gain, ("fsdp", "ctx"), axis=0, tiled=True),
        lax.all_gather(ln1_bias, ("fsdp", "ctx"), axis=0, tiled=True),
        lax.all_gather(ln2_gain, ("fsdp", "ctx"), axis=0, tiled=True),
        lax.all_gather(ln2_bias, ("fsdp", "ctx"), axis=0, tiled=True),
    )
    qkv_full, dense_full, up_full, down_full = (gathered[0], gathered[1], gathered[2], gathered[3])
    dense_shift = gathered[4].astype(jnp.float32)
    down_shift = gathered[5].astype(jnp.float32)
    gain_one = gathered[6].astype(jnp.float32)
    shift_one = gathered[7].astype(jnp.float32)
    gain_two = gathered[8].astype(jnp.float32)
    shift_two = gathered[9].astype(jnp.float32)
    p_rows = x_prompt.shape[1]
    cont_count = x_cont.shape[1]
    cont_len = x_cont.shape[2]
    model_width = x_prompt.shape[2]
    row_count = p_rows + cont_count * cont_len
    prompt_len = p_rows * lax.axis_size("ctx")
    local_cols = qkv_full.shape[2]
    head_count = local_cols // HD
    piece_index = lax.axis_index("ctx")
    inputs = jnp.concatenate(
        [x_prompt[0], x_cont[0].reshape(cont_count * cont_len, model_width)], axis=0
    ).astype(jnp.float32)
    offsets = jnp.arange(cont_len, dtype=jnp.int32)
    prompt_pos = piece_index * p_rows + jnp.arange(p_rows, dtype=jnp.int32)
    starts = cont_start[0]
    cont_pos = (starts[:, None] + offsets[None, :]).reshape(cont_count * cont_len)
    positions = jnp.concatenate([prompt_pos, cont_pos])
    key_limit = jnp.concatenate([prompt_pos + 1, jnp.repeat(starts, cont_len)])
    own_slot = jnp.repeat(jnp.arange(cont_count, dtype=jnp.int32), cont_len)
    own_offs = jnp.tile(offsets, cont_count)
    query_slot = jnp.concatenate([jnp.full((p_rows,), -1, jnp.int32), own_slot])
    query_offs = jnp.concatenate([jnp.zeros((p_rows,), jnp.int32), own_offs])
    key_slot = jnp.concatenate([jnp.full((prompt_len,), -1, jnp.int32), own_slot])
    key_offs = jnp.concatenate([jnp.zeros((prompt_len,), jnp.int32), own_offs])
    cos_t, sin_t = rotary_tables(positions)
    cos_t = cos_t[:, None, :]
    sin_t = sin_t[:, None, :]
    row_mean = jnp.mean(inputs, axis=-1, keepdims=True)
    centered = inputs - row_mean
    scale = lax.rsqrt(jnp.mean(centered * centered, axis=-1, keepdims=True) + EPS)
    unit = centered * scale
    norm_one = unit * gain_one + shift_one
    norm_two = unit * gain_two + shift_two
    unit_low = unit.astype(jnp.bfloat16)
    ln_one = norm_one.astype(jnp.bfloat16)
    ln_two = norm_two.astype(jnp.bfloat16)
    qkv_flat = qkv_full.reshape(model_width, 3 * local_cols)
    projected = jnp.dot(ln_one, qkv_flat, preferred_element_type=jnp.float32) + qkv_bias.reshape(
        3 * local_cols
    ).astype(jnp.float32)
    projected = projected.reshape(row_count, 3, head_count, HD)
    queries = rotate(projected[:, 0], cos_t, sin_t).astype(jnp.bfloat16)
    keys_own = rotate(projected[:, 1], cos_t, sin_t).astype(jnp.bfloat16)
    values_own = projected[:, 2].astype(jnp.bfloat16)
    prompt_keys, prompt_values = (
        lax.all_gather(keys_own[:p_rows].reshape(p_rows, local_cols), "ctx", axis=0, tiled=True),
        lax.all_gather(values_own[:p_rows].reshape(p_rows, local_cols), "ctx", axis=0, tiled=True),
    )
    all_keys = jnp.concatenate(
        [prompt_keys.reshape(prompt_len, head_count, HD), keys_own[p_rows:]], axis=0
    )
    all_values = jnp.concatenate(
        [prompt_values.reshape(prompt_len, head_count, HD), values_own[p_rows:]], axis=0
    )
    scores = masked_scores(
        queries, all_keys, key_limit, query_slot, query_offs, prompt_len, key_slot, key_offs
    )
    highest = jnp.max(scores, axis=-1, keepdims=True)
    log_total = highest + jnp.log(jnp.sum(jnp.exp(scores - highest), axis=-1, keepdims=True))
    probs_low = jnp.exp(scores - log_total).astype(jnp.bfloat16)
    attended = jnp.einsum("hqk,khd->qhd", probs_low, all_values, preferred_element_type=jnp.float32)
    attended_low = attended.reshape(row_count, local_cols).astype(jnp.bfloat16)
    attn_part = jnp.dot(attended_low, dense_full, preferred_element_type=jnp.float32)
    hidden = jnp.dot(ln_two, up_full, preferred_element_type=jnp.float32) + fc1_bias.astype(
        jnp.float32
    )
    active_low = exact_gelu(hidden).astype(jnp.bfloat16)
    mlp_part = jnp.dot(active_low, down_full, preferred_element_type=jnp.float32)
    mixed = lax.psum((attn_part + mlp_part).astype(jnp.bfloat16), "tp").astype(jnp.float32)
    output = inputs + mixed + dense_shift + down_shift
    grad_out = jnp.concatenate(
        [dy_prompt[0], dy_cont[0].reshape(cont_count * cont_len, model_width)], axis=0
    )
    grad_dense = jnp.dot(attended_low.T, grad_out, preferred_element_type=jnp.float32)
    grad_down = jnp.dot(active_low.T, grad_out, preferred_element_type=jnp.float32)
    grad_shift = jnp.sum(grad_out.astype(jnp.float32), axis=0)
    grad_attended = (
        jnp.dot(grad_out, dense_full.T, preferred_element_type=jnp.float32)
        .astype(jnp.bfloat16)
        .reshape(row_count, head_count, HD)
    )
    scores = masked_scores(
        queries, all_keys, key_limit, query_slot, query_offs, prompt_len, key_slot, key_offs
    )
    probs = jnp.exp(scores - log_total)
    probs_low = probs.astype(jnp.bfloat16)
    grad_probs = jnp.einsum(
        "qhd,khd->hqk", grad_attended, all_values, preferred_element_type=jnp.float32
    )
    inner = jnp.sum(probs * grad_probs, axis=-1, keepdims=True)
    grad_scores = (probs * (grad_probs - inner)).astype(jnp.bfloat16)
    grad_queries = (
        jnp.einsum("hqk,khd->qhd", grad_scores, all_keys, preferred_element_type=jnp.float32)
        * 0.125
    )
    grad_keys = (
        jnp.einsum("hqk,qhd->khd", grad_scores, queries, preferred_element_type=jnp.float32) * 0.125
    )
    grad_values = jnp.einsum(
        "hqk,qhd->khd", probs_low, grad_attended, preferred_element_type=jnp.float32
    )
    prompt_key_grads, prompt_value_grads = (
        lax.psum_scatter(
            grad_keys[:prompt_len].reshape(prompt_len, local_cols).astype(jnp.bfloat16),
            "ctx",
            scatter_dimension=0,
            tiled=True,
        ),
        lax.psum_scatter(
            grad_values[:prompt_len].reshape(prompt_len, local_cols).astype(jnp.bfloat16),
            "ctx",
            scatter_dimension=0,
            tiled=True,
        ),
    )
    grad_keys = jnp.concatenate(
        [
            prompt_key_grads.reshape(p_rows, head_count, HD).astype(jnp.float32),
            grad_keys[prompt_len:],
        ],
        axis=0,
    )
    grad_values = jnp.concatenate(
        [
            prompt_value_grads.reshape(p_rows, head_count, HD).astype(jnp.float32),
            grad_values[prompt_len:],
        ],
        axis=0,
    )
    grad_projected = jnp.stack(
        [rotate(grad_queries, cos_t, -sin_t), rotate(grad_keys, cos_t, -sin_t), grad_values], axis=1
    )
    grad_proj_low = grad_projected.reshape(row_count, 3 * local_cols).astype(jnp.bfloat16)
    moment_one = jnp.dot(unit_low.T, grad_proj_low, preferred_element_type=jnp.float32)
    grad_qkv_bias = jnp.sum(grad_proj_low.astype(jnp.float32), axis=0)
    grad_norm_one = jnp.dot(grad_proj_low, qkv_flat.T, preferred_element_type=jnp.float32)
    grad_active = jnp.dot(grad_out, down_full.T, preferred_element_type=jnp.float32)
    gelu_back = jax.vjp(exact_gelu, hidden)[1]
    grad_hidden_low = gelu_back(grad_active)[0].astype(jnp.bfloat16)
    moment_two = jnp.dot(unit_low.T, grad_hidden_low, preferred_element_type=jnp.float32)
    grad_up_bias = jnp.sum(grad_hidden_low.astype(jnp.float32), axis=0)
    grad_norm_two = jnp.dot(grad_hidden_low, up_full.T, preferred_element_type=jnp.float32)
    turned = (grad_norm_one * gain_one + grad_norm_two * gain_two).astype(jnp.bfloat16)
    turned = lax.psum(turned, "tp").astype(jnp.float32)
    grad_inputs = grad_out.astype(jnp.float32) + scale * (
        turned
        - jnp.mean(turned, axis=-1, keepdims=True)
        - unit * jnp.mean(turned * unit, axis=-1, keepdims=True)
    )
    both = ("fsdp", "ctx")

    def scatter(array, axis):
        return lax.psum_scatter(
            array.astype(jnp.bfloat16), both, scatter_dimension=axis, tiled=True
        ).astype(jnp.float32)

    own_one = scatter(moment_one, 0)
    own_two = scatter(moment_two, 0)
    d_dense = scatter(grad_dense, 1)
    d_down = scatter(grad_down, 1)
    bias_qkv_total, bias_up_total, shift_total = lax.psum(
        (grad_qkv_bias, grad_up_bias, grad_shift), both
    )
    own_rows = w_qkv.shape[0]
    own_place = (lax.axis_index("fsdp") * lax.axis_size("ctx") + piece_index) * own_rows
    d_shift = lax.dynamic_slice_in_dim(shift_total, own_place, own_rows)
    own_qkv = w_qkv.reshape(own_rows, 3 * local_cols).astype(jnp.float32)
    own_up = w_fc1.astype(jnp.float32)
    small = lax.psum(
        jnp.stack(
            [
                jnp.sum(own_one * own_qkv, axis=1),
                jnp.sum(own_qkv * bias_qkv_total, axis=1),
                jnp.sum(own_two * own_up, axis=1),
                jnp.sum(own_up * bias_up_total, axis=1),
            ]
        ),
        "tp",
    )
    d_qkv = (
        own_one * ln1_gain.astype(jnp.float32)[:, None]
        + ln1_bias.astype(jnp.float32)[:, None] * bias_qkv_total
    ).reshape(own_rows, 3, local_cols)
    d_up = (
        own_two * ln2_gain.astype(jnp.float32)[:, None]
        + ln2_bias.astype(jnp.float32)[:, None] * bias_up_total
    )
    y_prompt = output[:p_rows][None]
    y_cont = output[p_rows:].reshape(1, cont_count, cont_len, model_width)
    dx_prompt = grad_inputs[:p_rows][None]
    dx_cont = grad_inputs[p_rows:].reshape(1, cont_count, cont_len, model_width)
    return (
        y_prompt,
        y_cont,
        dx_prompt,
        dx_cont,
        d_qkv,
        bias_qkv_total.reshape(3, local_cols),
        d_dense,
        d_shift,
        d_up,
        bias_up_total,
        d_down,
        d_shift,
        small[0],
        small[1],
        small[2],
        small[3],
    )


def solution(mesh):
    placed = (
        P("fsdp", "ctx", None),
        P("fsdp", "ctx", None, None),
        P("fsdp", "ctx"),
        P(("fsdp", "ctx"), None, "tp"),
        P(None, "tp"),
        P("tp", ("fsdp", "ctx")),
        P(("fsdp", "ctx")),
        P(("fsdp", "ctx"), "tp"),
        P("tp"),
        P("tp", ("fsdp", "ctx")),
        P(("fsdp", "ctx")),
        P(("fsdp", "ctx")),
        P(("fsdp", "ctx")),
        P(("fsdp", "ctx")),
        P(("fsdp", "ctx")),
        P("fsdp", "ctx", None),
        P("fsdp", "ctx", None, None),
    )
    return jax.shard_map(
        on_device,
        mesh=mesh,
        in_specs=placed,
        out_specs=(
            P("fsdp", "ctx", None),
            P("fsdp", "ctx", None, None),
            P("fsdp", "ctx", None),
            P("fsdp", "ctx", None, None),
            P(("fsdp", "ctx"), None, "tp"),
            P(None, "tp"),
            P("tp", ("fsdp", "ctx")),
            P(("fsdp", "ctx")),
            P(("fsdp", "ctx"), "tp"),
            P("tp"),
            P("tp", ("fsdp", "ctx")),
            P(("fsdp", "ctx")),
            P(("fsdp", "ctx")),
            P(("fsdp", "ctx")),
            P(("fsdp", "ctx")),
            P(("fsdp", "ctx")),
        ),
        check_vma=False,
    )
```

profile of v0, /device:TPU:0, one launch (start us, length us, event | category | flops | bytes accessed | tf_op | source)
XLA Modules:
  0.0 632.3 jit_solution(4390822750926472987)
XLA Ops:
  7.3 1.9 copy.40
  10.9 1.9 convert_reduce_fusion.1
  12.8 1.7 fusion.15
  14.6 14.7 %all-gather = bf16[8,1,128]{2,1,0:T(2,128)(2,1)S(1)} all-gather(bf16[1,1,128]{2,1,0:T(2,128)(2,1)S(1)} %bitcast.164), channel_id=1, replica_groups=mesh['fsdp'=2,'ctx'=4,'tp'=4] {'fsdp','ctx'}, dimensions={0}, use_global_device_ids=true | all-gather | bytes 2304 | tf_op jit(solution)/shard_map/all_gather | solution.py:73
  29.3 13.2 %all-gather.1 = bf16[8,1,128]{2,1,0:T(2,128)(2,1)S(1)} all-gather(bf16[1,1,128]{2,1,0:T(2,128)(2,1)S(1)} %bitcast.165), channel_id=1, replica_groups=mesh['fsdp'=2,'ctx'=4,'tp'=4] {'fsdp','ctx'}, dimensions={0}, use_global_device_ids=true | all-gather | bytes 2304 | tf_op jit(solution)/shard_map/all_gather | solution.py:74
  44.1 24.7 %all_gather.41 = bf16[256,1024]{1,0:T(8,128)(2,1)S(1)} all-gather(bf16[256,128]{1,0:T(8,128)(2,1)S(1)} %copy-done.30), channel_id=1, replica_groups=mesh['fsdp'=2,'ctx'=4,'tp'=4] {'fsdp','ctx'}, dimensions={1}, use_global_device_ids=true | all-gather | bytes 589824 | tf_op jit(solution)/shard_map/all_gather | solution.py:68
  68.9 13.9 %all-gather.2 = bf16[8,1,128]{2,1,0:T(2,128)(2,1)S(1)} all-gather(bf16[1,1,128]{2,1,0:T(2,128)(2,1)S(1)} %bitcast.162), channel_id=1, replica_groups=mesh['fsdp'=2,'ctx'=4,'tp'=4] {'fsdp','ctx'}, dimensions={0}, use_global_device_ids=true | all-gather | bytes 2304 | tf_op jit(solution)/shard_map/all_gather | solution.py:75
  83.9 13.2 %all-gather.3 = bf16[8,1,128]{2,1,0:T(2,128)(2,1)S(1)} all-gather(bf16[1,1,128]{2,1,0:T(2,128)(2,1)S(1)} %bitcast.163), channel_id=1, replica_groups=mesh['fsdp'=2,'ctx'=4,'tp'=4] {'fsdp','ctx'}, dimensions={0}, use_global_device_ids=true | all-gather | bytes 2304 | tf_op jit(solution)/shard_map/all_gather | solution.py:76
  97.7 2.6 convolution_convert_fusion.5
  100.3 3.0 fusion.2
  103.4 3.6 fusion.40
  108.2 13.2 %all_gather.40 = bf16[1024,256]{0,1:T(8,128)(2,1)S(1)} all-gather(bf16[256,256]{0,1:T(8,128)(2,1)S(1)} %bitcast.143), channel_id=1, replica_groups=mesh['fsdp'=2,'ctx'=4,'tp'=4] {'ctx'}, dimensions={0}, use_global_device_ids=true | all-gather | bytes 655360 | tf_op jit(solution)/shard_map/all_gather | solution.py:130
  121.4 12.8 %fusion = (f32[4,1024]{1,0:T(4,128)S(1)}, f32[4,1024,1792]{2,1,0:T(8,128)}) fusion(pred[1024,1792]{1,0:T(8,128)(4,1)S(1)} %fusion.2, bf16[1024,4,48]{0,2,1:T(8,128)(2,1)S(1)} %slice.242, bf16[1024,4,16]{0,2,1:T(8,128)(2,1)S(1)} %get-tuple-element.95, bf16[1024,4,64]{0,2,1:T(8,128)(2,1)S(1)} %bitcast.121, bf16[1024,4,48]{0,2,1:T(8,128)(2,1)S(1)} %slice.243, ...), kind=kOutput, calls=%fused_computation.5 | convolution fusion | flops 966717440 | bytes 32784384 | tf_op jit(solution)/shard_map/qhd,khd->hqk/dot_general | solution.py:37
  134.2 13.8 %exponential_reduce_fusion = f32[4,1024]{1,0:T(4,128)S(1)} fusion(f32[4,1024,1792]{2,1,0:T(8,128)} %get-tuple-element.107, f32[4,1024]{1,0:T(4,128)S(1)} %get-tuple-element.106, pred[1024,1792]{1,0:T(8,128)(4,1)S(1)} %fusion.2), kind=kLoop, calls=%fused_computation.3 | loop fusion | flops 29356032 | bytes 31227904 | tf_op jit(solution)/shard_map/reduce_sum | solution.py:143
  148.0 12.0 %all_gather.39 = bf16[1024,256]{0,1:T(8,128)(2,1)S(1)} all-gather(bf16[256,256]{0,1:T(8,128)(2,1)S(1)} %bitcast.144), channel_id=1, replica_groups=mesh['fsdp'=2,'ctx'=4,'tp'=4] {'ctx'}, dimensions={0}, use_global_device_ids=true | all-gather | bytes 655360 | tf_op jit(solution)/shard_map/all_gather | solution.py:131
  160.1 22.0 %multiply_reduce_fusion = (f32[4,1024]{1,0:T(4,128)S(1)}, f32[4,1024,1792]{2,1,0:T(8,128)}) fusion(f32[4,1024,1792]{2,1,0:T(8,128)} %get-tuple-element.107, f32[4,1024]{1,0:T(4,128)S(1)} %log_add_fusion, pred[1024,1792]{1,0:T(8,128)(4,1)S(1)} %fusion.2, bf16[1024,4,64]{0,2,1:T(8,128)(2,1)S(1)} %bitcast.135, bf16[768,4,64]{0,2,1:T(8,128)(2,1)S(1)} %slice_bitcast_fusion.4, ...), kind=kOutput, calls=%fused_computation.1 | convolution fusion | flops 978055168 | bytes 62029824 | tf_op jit(solution)/shard_map/qhd,khd->hqk/dot_general | solution.py:171
  182.1 24.7 %multiply_convert_fusion = bf16[4,1024,1792]{2,1,0:T(8,128)(2,1)} fusion(f32[4,1024,1792]{2,1,0:T(8,128)} %get-tuple-element.109, f32[4,1024,1792]{2,1,0:T(8,128)} %get-tuple-element.107, f32[4,1024]{1,0:T(4,128)S(1)} %get-tuple-element.108, f32[4,1024]{1,0:T(4,128)S(1)} %log_add_fusion, pred[1024,1792]{1,0:T(8,128)(4,1)S(1)} %fusion.2), kind=kLoop, calls=%fused_computation | loop fusion | flops 44040192 | bytes 75268096 | tf_op jit(solution)/shard_map/convert_element_type | solution.py:175
  206.8 7.8 %fusion.25 = f32[1792,4,64]{0,2,1:T(8,128)S(1)} fusion(bf16[4,1024,1792]{2,1,0:T(8,128)(2,1)} %multiply_convert_fusion, bf16[1024,4,48]{0,2,1:T(8,128)(2,1)S(1)} %slice.243, bf16[1024,4,16]{0,2,1:T(8,128)(2,1)S(1)} %get-tuple-element.96), kind=kOutput, calls=%fused_computation.57 | convolution fusion | flops 941031424 | bytes 17039360 | tf_op jit(solution)/shard_map/hqk,qhd->khd/dot_general | solution.py:181
  214.6 0.9 slice.241
  215.5 0.9 slice.176
  216.4 14.1 %convolution_convert_fusion.3 = bf16[4,64,1024]{2,1,0:T(8,128)(2,1)} fusion(bf16[768,4,64]{0,2,1:T(8,128)(2,1)} %copy-done.13, bf16[1024,4,64]{0,2,1:T(8,128)(2,1)} %bitcast.120, f32[4,1024,1792]{2,1,0:T(8,128)} %get-tuple-element.107, f32[4,1024]{1,0:T(4,128)S(1)} %log_add_fusion, pred[1024,1792]{1,0:T(8,128)(4,1)S(1)} %fusion.2), kind=kOutput, calls=%fused_computation.83 | convolution fusion | flops 970981376 | bytes 32653312 | tf_op jit(solution)/shard_map/hqk,khd->qhd/dot_general | solution.py:145
  230.8 13.7 %convolution_bitcast_fusion = bf16[1792,4,64]{0,2,1:T(8,128)(2,1)S(1)} fusion(bf16[1024,4,64]{0,2,1:T(8,128)(2,1)} %bitcast.134, f32[4,1024,1792]{2,1,0:T(8,128)} %get-tuple-element.107, f32[4,1024]{1,0:T(4,128)S(1)} %log_add_fusion, pred[1024,1792]{1,0:T(8,128)(4,1)S(1)} %fusion.2), kind=kOutput, calls=%fused_computation.56 | convolution fusion | flops 968884224 | bytes 32653312 | tf_op jit(solution)/shard_map/hqk,qhd->khd/dot_general | solution.py:183
  244.5 0.9 slice.240
  246.2 10.2 %fusion.43 = f32[1024,4,64]{0,2,1:T(8,128)S(1)} fusion(bf16[4,1024,1792]{2,1,0:T(8,128)(2,1)} %multiply_convert_fusion, bf16[1024,4,48]{0,2,1:T(8,128)(2,1)} %copy-done.6, bf16[1024,4,16]{0,2,1:T(8,128)(2,1)S(1)} %get-tuple-element.95, bf16[1024,4,64]{0,2,1:T(8,128)(2,1)} %bitcast.122), kind=kOutput, calls=%fused_computation.82 | convolution fusion | flops 943915008 | bytes 16777216 | tf_op jit(solution)/shard_map/hqk,khd->qhd/dot_general | solution.py:177
  256.4 1.0 copy-done.5
  257.4 0.8 slice.174
  258.2 1.5 convolution_convert_fusion.4
  259.8 2.1 copy.45
  261.8 1.6 slice_negate_fusion
  263.6 16.0 %multiply_convert_fusion.1 = (bf16[1024,1024]{1,0:T(8,128)(2,1)S(1)}, f32[1024,1024]{1,0:T(8,128)}, f32[1024,1024]{1,0:T(8,128)}) fusion(f32[1024]{0:T(1024)S(1)} %copy-done.37, bf16[1024,1024]{1,0:T(8,128)(2,1)} %all-gather.12.cloned.1.call-done, f32[1024]{0:T(1024)S(1)} %bitcast.155, f32[1024]{0:T(1024)S(1)} %bitcast.153, f32[1024]{0:T(1024)S(1)} %copy-done.34, ...), kind=kOutput, calls=%fused_computation.39 | convolution fusion | flops 2226126848 | bytes 14700544 | tf_op jit(solution)/shard_map/dot_general | solution.py:148
  279.6 1.3 copy-done.60
  280.9 3.8 convolution_convert_fusion
  284.7 3.9 copy.47
  289.2 4.7 fusion.80
  293.9 2.1 add_convert_fusion.2
  296.0 0.9 copy-done.57
  296.9 5.2 convert_reduce_fusion.3
  302.2 1.0 convert.34
  303.2 1.0 fusion.59
  304.4 1.2 maximum_bitcast_fusion.1
  306.0 1.9 fusion.81
  308.7 3.8 add_convert_fusion
  312.7 5.8 convolution_convert_fusion.1
  318.6 12.5 %all-gather.4 = bf16[8,1,128]{2,1,0:T(2,128)(2,1)S(1)} all-gather(bf16[1,1,128]{2,1,0:T(2,128)(2,1)S(1)} %bitcast.166), channel_id=1, replica_groups=mesh['fsdp'=2,'ctx'=4,'tp'=4] {'fsdp','ctx'}, dimensions={0}, use_global_device_ids=true | all-gather | bytes 2304 | tf_op jit(solution)/shard_map/all_gather | solution.py:71
  331.1 13.4 %all-gather.5 = bf16[8,1,128]{2,1,0:T(2,128)(2,1)S(1)} all-gather(bf16[1,1,128]{2,1,0:T(2,128)(2,1)S(1)} %bitcast.167), channel_id=1, replica_groups=mesh['fsdp'=2,'ctx'=4,'tp'=4] {'fsdp','ctx'}, dimensions={0}, use_global_device_ids=true | all-gather | bytes 2304 | tf_op jit(solution)/shard_map/all_gather | solution.py:72
  344.7 0.9 copy.46
  346.4 4.8 convolution_convert_fusion.2
  351.2 14.9 %reduce-scatter.21.cloned.1.call-done = bf16[128,1024]{1,0:T(8,128)(2,1)} async-done(((bf16[1024,1024]{1,0:T(8,128)(2,1)}), bf16[128,1024]{1,0:T(8,128)(2,1)}) %reduce-scatter.21.cloned.1.call-update) | async-done | bytes 262160
  366.1 1.1 copy.48
  367.2 0.8 convert_element_type.240
  368.1 156.4 %all-reduce.8.cloned.1.call-done = (bf16[1024,1024]{1,0:T(8,128)(2,1)}, bf16[1024,1024]{1,0:T(8,128)(2,1)}) async-done(((bf16[1024,1024]{1,0:T(8,128)(2,1)}, bf16[1024,1024]{1,0:T(8,128)(2,1)}), (bf16[1024,1024]{1,0:T(8,128)(2,1)}, bf16[1024,1024]{1,0:T(8,128)(2,1)})) %all-reduce.8.cloned.1.call-update) | async-done | bytes 4194320 | tf_op jit(solution)/shard_map/psum | solution.py:153
  524.5 3.7 convert_reduce_fusion
  528.2 6.2 convert_reduce_fusion.2
  534.4 26.8 %all-reduce.4 = (f32[768]{0:T(1024)S(1)}, f32[1024]{0:T(1024)S(1)}, f32[1024]{0:T(1024)S(1)}) all-reduce(f32[768]{0:T(1024)S(1)} %reduce_sum.126, f32[1024]{0:T(1024)S(1)} %get-tuple-element.79, f32[1024]{0:T(1024)S(1)} %get-tuple-element.110), channel_id=1, replica_groups=mesh['fsdp'=2,'ctx'=4,'tp'=4] {'fsdp','ctx'}, use_global_device_ids=true, to_apply=%region_13.14 | all-reduce | flops 2816 | bytes 22528 | tf_op jit(solution)/shard_map/psum | solution.py:245
  561.3 4.3 slice.170
  565.6 1.9 slice.186
  567.6 1.0 reduce-scatter.17.cloned.1.call-done
  568.7 2.0 fusion.51
  570.7 2.3 slice_bitcast_fusion
  573.0 2.3 slice_bitcast_fusion.1
  575.3 35.0 %reduce-scatter.15.cloned.1.call-done = bf16[128,768]{1,0:T(8,128)(2,1)} async-done(((bf16[1024,768]{1,0:T(8,128)(2,1)}), bf16[128,768]{1,0:T(8,128)(2,1)}) %reduce-scatter.15.cloned.1.call-update) | async-done | bytes 196624 | tf_op jit(solution)/shard_map/reduce_scatter | solution.py:237
  610.3 1.1 fusion.54
  611.4 11.7 %psum.47 = f32[4,128]{1,0:T(4,128)S(1)} all-reduce(f32[4,128]{1,0:T(4,128)S(1)} %pad_maximum_fusion.11), channel_id=1, replica_groups=mesh['fsdp'=2,'ctx'=4,'tp'=4] {'tp'}, use_global_device_ids=true, to_apply=%region_25.26 | all-reduce | flops 512 | bytes 4096 | tf_op jit(solution)/shard_map/psum | solution.py:253
  623.8 0.9 copy.44
  (211 shorter events, 12.0 us)
Async XLA Ops:
  7.2 5.6 copy-start
  7.2 7.4 %copy-start.50 = (bf16[128]{0:T(256)(128)(2,1)S(1)}, bf16[128]{0:T(256)(128)(2,1)}, u32[]{:S(2)}) copy-start(bf16[128]{0:T(256)(128)(2,1)} %param.28) | copy-start | bytes 772
  7.2 22.1 %copy-start.52 = (bf16[128]{0:T(256)(128)(2,1)S(1)}, bf16[128]{0:T(256)(128)(2,1)}, u32[]{:S(2)}) copy-start(bf16[128]{0:T(256)(128)(2,1)} %param.29) | copy-start | bytes 772
  7.2 35.3 %copy-start.43 = (bf16[3,256]{1,0:T(4,128)(2,1)S(1)}, bf16[3,256]{1,0:T(4,128)(2,1)}, u32[]{:S(2)}) copy-start(bf16[3,256]{1,0:T(4,128)(2,1)} %param.21) | copy-start | bytes 4612
  7.2 35.3 %copy-start.45 = (s32[1,3]{1,0:T(1,128)S(1)}, s32[1,3]{1,0:T(1,128)}, u32[]{:S(2)}) copy-start(s32[1,3]{1,0:T(1,128)} %param.19) | copy-start | bytes 40
  7.2 36.9 %copy-start.30 = (bf16[256,128]{1,0:T(8,128)(2,1)S(1)}, bf16[256,128]{1,0:T(8,128)(2,1)}, u32[]{:S(2)}) copy-start(bf16[256,128]{1,0:T(8,128)(2,1)} %param.22) | copy-start | bytes 196612
  7.2 61.6 %copy-start.46 = (bf16[128]{0:T(256)(128)(2,1)S(1)}, bf16[128]{0:T(256)(128)(2,1)}, u32[]{:S(2)}) copy-start(bf16[128]{0:T(256)(128)(2,1)} %param.30) | copy-start | bytes 772
  7.3 76.0 %copy-start.44 = (bf16[1024]{0:T(1024)(128)(2,1)S(1)}, bf16[1024]{0:T(1024)(128)(2,1)}, u32[]{:S(2)}) copy-start(bf16[1024]{0:T(1024)(128)(2,1)} %param.25) | copy-start | bytes 6148
  7.3 76.6 %copy-start.48 = (bf16[128]{0:T(256)(128)(2,1)S(1)}, bf16[128]{0:T(256)(128)(2,1)}, u32[]{:S(2)}) copy-start(bf16[128]{0:T(256)(128)(2,1)} %param.31) | copy-start | bytes 772
  7.3 90.5 %copy-start.14 = (bf16[1,3,256,1024]{3,2,1,0:T(8,128)(2,1)S(1)}, bf16[1,3,256,1024]{3,2,1,0:T(8,128)(2,1)}, u32[]{:S(2)}) copy-start(bf16[1,3,256,1024]{3,2,1,0:T(8,128)(2,1)} %param.33) | copy-start | bytes 4718596
  7.3 96.0 %all-gather.10.cloned.1.call-start = ((), (), s32[]{:S(2)}) async-start(), calls=%async_computation.6 | async-start | bytes 1769472 | tf_op jit(solution)/shard_map/all_gather | solution.py:67
  9.3 254.3 %all-gather.12.cloned.1.call-start = ((), (), s32[]{:S(2)}) async-start(), calls=%async_computation.7 | async-start | bytes 2359296 | tf_op jit(solution)/shard_map/all_gather | solution.py:69
  10.0 279.1 %all-gather.14.cloned.1.call-start = ((), (), s32[]{:S(2)}) async-start(), calls=%async_computation.8 | async-start | bytes 2359296 | tf_op jit(solution)/shard_map/all_gather | solution.py:70
  10.8 291.4 %reduce-scatter.11.cloned.1.call-start = ((), (), s32[]{:S(2)}) async-start(), calls=%async_computation.9 | async-start | bytes 655360 | tf_op jit(solution)/shard_map/reduce_scatter | solution.py:187
  12.8 90.5 %copy-start.31 = (f32[1024]{0:T(1024)}, f32[1024]{0:T(1024)S(1)}, u32[]{:S(2)}) copy-start(f32[1024]{0:T(1024)S(1)} %broadcast_multiply_fusion.2) | copy-start | bytes 12292
  14.6 88.8 %copy-start.33 = (f32[1024]{0:T(1024)}, f32[1024]{0:T(1024)S(1)}, u32[]{:S(2)}) copy-start(f32[1024]{0:T(1024)S(1)} %add_rsqrt_fusion) | copy-start | bytes 12292
  29.3 74.1 %copy-start.38 = (f32[8,1,128]{2,1,0:T(1,128)}, f32[8,1,128]{2,1,0:T(1,128)S(1)}, u32[]{:S(2)}) copy-start(f32[8,1,128]{2,1,0:T(1,128)S(1)} %convert_element_type.249) | copy-start | bytes 12292
  68.9 28.9 %copy-start.9 = (bf16[256,1024]{1,0:T(8,128)(2,1)}, bf16[256,1024]{1,0:T(8,128)(2,1)S(1)}, u32[]{:S(2)}) copy-start(bf16[256,1024]{1,0:T(8,128)(2,1)S(1)} %all_gather.41) | copy-start | bytes 1572868
  107.3 14.1 %copy-start.6 = (bf16[1024,4,48]{0,2,1:T(8,128)(2,1)}, bf16[1024,4,48]{0,2,1:T(8,128)(2,1)S(1)}, u32[]{:S(2)}) copy-start(bf16[1024,4,48]{0,2,1:T(8,128)(2,1)S(1)} %slice.242) | copy-start | bytes 1179652
  107.7 52.4 %copy-start.13 = (bf16[768,4,64]{0,2,1:T(8,128)(2,1)}, bf16[768,4,64]{0,2,1:T(8,128)(2,1)S(1)}, u32[]{:S(2)}) copy-start(bf16[768,4,64]{0,2,1:T(8,128)(2,1)S(1)} %slice_bitcast_fusion.4) | copy-start | bytes 1179652
  121.4 12.9 %copy-start.12 = (bf16[1024,256]{0,1:T(8,128)(2,1)}, bf16[1024,256]{0,1:T(8,128)(2,1)S(1)}, u32[]{:S(2)}) copy-start(bf16[1024,256]{0,1:T(8,128)(2,1)S(1)} %all_gather.40) | copy-start | bytes 1572868
  134.2 25.9 %copy-start.23 = (bf16[1024,256]{0,1:T(8,128)(2,1)S(1)}, bf16[1024,256]{0,1:T(8,128)(2,1)}, u32[]{:S(2)}) copy-start(bf16[1024,256]{0,1:T(8,128)(2,1)} %convolution_convert_fusion.5) | copy-start | bytes 1572868
  160.1 22.1 %copy-start.8 = (bf16[1024,256]{0,1:T(8,128)(2,1)}, bf16[1024,256]{0,1:T(8,128)(2,1)S(1)}, u32[]{:S(2)}) copy-start(bf16[1024,256]{0,1:T(8,128)(2,1)S(1)} %all_gather.39) | copy-start | bytes 1572868
  230.6 73.8 %reduce-scatter.13.cloned.1.call-start = ((), (), s32[]{:S(2)}) async-start(), calls=%async_computation.10 | async-start | bytes 655360 | tf_op jit(solution)/shard_map/reduce_scatter | solution.py:193
  246.2 12.1 %copy-start.24 = (bf16[4,64,1024]{2,1,0:T(8,128)(2,1)S(1)}, bf16[4,64,1024]{2,1,0:T(8,128)(2,1)}, u32[]{:S(2)}) copy-start(bf16[4,64,1024]{2,1,0:T(8,128)(2,1)} %convolution_convert_fusion.3) | copy-start | bytes 1572868
  246.2 12.1 %copy-start.25 = (bf16[1,256,1024]{2,1,0:T(8,128)(2,1)S(1)}, bf16[1,256,1024]{2,1,0:T(8,128)(2,1)}, u32[]{:S(2)}) copy-start(bf16[1,256,1024]{2,1,0:T(8,128)(2,1)} %param.32) | copy-start | bytes 1572868
  246.2 98.5 %reduce-scatter.19.cloned.1.call-start = ((), (), s32[]{:S(2)}) async-start(), calls=%async_computation.13 | async-start | bytes 589824
  246.2 12.0 %copy-start.15 = (bf16[1,3,256,1024]{3,2,1,0:T(8,128)(2,1)S(1)}, bf16[1,3,256,1024]{3,2,1,0:T(8,128)(2,1)}, u32[]{:S(2)}) copy-start(bf16[1,3,256,1024]{3,2,1,0:T(8,128)(2,1)} %param.33) | copy-start | bytes 4718596
  257.4 6.2 copy-start.4
  257.4 6.2 copy-start.32
  257.4 6.2 copy-start.34
  257.4 6.2 copy-start.37
  257.4 6.2 copy-start.40
  257.4 6.2 copy-start.42
  263.5 102.6 %reduce-scatter.21.cloned.1.call-start = ((), (), s32[]{:S(2)}) async-start(), calls=%async_computation.14 | async-start | bytes 2359296
  263.6 17.3 %copy-start.16 = (bf16[1,3,256,1024]{3,2,1,0:T(8,128)(2,1)S(1)}, bf16[1,3,256,1024]{3,2,1,0:T(8,128)(2,1)}, u32[]{:S(2)}) copy-start(bf16[1,3,256,1024]{3,2,1,0:T(8,128)(2,1)} %param.33) | copy-start | bytes 4718596
  288.6 5.2 copy-start.10
  288.7 235.8 %all-reduce.8.cloned.1.call-start = ((), (), s32[]{:S(2)}) async-start(), calls=%async_computation.15 | async-start | bytes 8388608 | tf_op jit(solution)/shard_map/psum | solution.py:153
  289.1 6.8 %copy-start.61 = (f32[1024,1024]{1,0:T(8,128)S(1)}, f32[1024,1024]{1,0:T(8,128)}, u32[]{:S(2)}) copy-start(f32[1024,1024]{1,0:T(8,128)} %get-tuple-element.76) | copy-start | bytes 12582916
  289.2 6.8 %copy-start.62 = (f32[1024,1024]{1,0:T(8,128)S(1)}, f32[1024,1024]{1,0:T(8,128)}, u32[]{:S(2)}) copy-start(f32[1024,1024]{1,0:T(8,128)} %get-tuple-element.105) | copy-start | bytes 12582916
  293.9 2.1 copy-start.17
  293.9 3.0 copy-start.57
  296.9 6.2 copy-start.2
  296.9 6.3 copy-start.22
  296.9 6.3 copy-start.27
  296.9 6.3 copy-start.28
  302.2 2.2 copy-start.18
  306.0 2.1 copy-start.56
  306.0 2.7 copy-start.63
  312.5 6.0 copy-start.47
  312.6 6.0 copy-start.49
  312.6 6.0 copy-start.51
  312.6 6.0 copy-start.53
  312.6 6.0 copy-start.54
  312.6 18.5 %copy-start.55 = (bf16[128]{0:T(256)(128)(2,1)S(1)}, bf16[128]{0:T(256)(128)(2,1)}, u32[]{:S(2)}) copy-start(bf16[128]{0:T(256)(128)(2,1)} %param.27) | copy-start | bytes 772
  312.6 31.9 %copy-start.7 = (bf16[128,3,256]{0,2,1:T(8,128)(2,1)S(1)}, bf16[128,3,256]{0,2,1:T(8,128)(2,1)}, u32[]{:S(2)}) copy-start(bf16[128,3,256]{0,2,1:T(8,128)(2,1)} %copy.40) | copy-start | bytes 589828
  312.6 256.1 %reduce-scatter.17.cloned.1.call-start = ((), (), s32[]{:S(2)}) async-start(), calls=%async_computation.12 | async-start | bytes 2359296 | tf_op jit(solution)/shard_map/reduce_scatter | solution.py:237
  318.5 291.8 %reduce-scatter.15.cloned.1.call-start = ((), (), s32[]{:S(2)}) async-start(), calls=%async_computation.11 | async-start | bytes 1769472 | tf_op jit(solution)/shard_map/reduce_scatter | solution.py:237
  524.5 3.7 copy-start.3
  524.5 3.8 copy-start.11
  561.3 7.4 %copy-start.36 = (f32[1024]{0:T(1024)}, f32[1024]{0:T(1024)S(1)}, u32[]{:S(2)}) copy-start(f32[1024]{0:T(1024)S(1)} %get-tuple-element.141) | copy-start | bytes 12292
  561.3 6.2 copy-start.35
  561.3 4.3 copy-start.1
  565.6 3.1 copy-start.20
  (10 other events, 14.0 us)
Sparse Core Ops, SparseCore 0:
  10.0 28.5 all-gather.9
  40.5 32.9 all-gather.11
  75.4 27.9 all-gather.13
  230.7 25.1 reduce-scatter.10
  259.4 24.7 reduce-scatter.12
  287.1 34.0 reduce-scatter.18
  324.9 41.2 reduce-scatter.20
  369.1 155.3 all-reduce.7
  528.1 40.5 reduce-scatter.16
  571.8 38.4 reduce-scatter.14
where the time goes:
time: 641 us; the launch traced here: 632 us
  waiting for transfers between devices  209 us (33%)
  blocking collectives  169 us (26%)
  matrix products  136 us (21%)
  other arithmetic  68.7 us (11%)
  local copies, waits for them, and re-layouts  32.7 us (5%)
  between operations  15.3 us (2%)
    psum x1, waiting for transfers between devices, on_device(): lax.psum((attn_part + mlp_part).astype(jnp.bfloat16), 'tp')  156 us
    reduce_scatter x2, waiting for transfers between devices, scatter(): lax.psum_scatter(array.astype(jnp.bfloat16), both, scatter_dimension=axis...  36 us
    psum x1, blocking collectives, on_device(): lax.psum((grad_qkv_bias, grad_up_bias, grad_shift), both)  26.8 us
    all_gather x1, blocking collectives, on_device(): lax.all_gather(w_dense, ('fsdp', 'ctx'), axis=1, tiled=True)  24.7 us
    convert_element_type x1, other arithmetic, on_device(): grad_scores = (probs * (grad_probs - inner)).astype(jnp.bfloat16)  24.7 us
    dot_general x1, matrix products, on_device(): jnp.einsum('qhd,khd->hqk', grad_attended, all_values, preferred_element_t...  22 us
    unnamed x12, waiting for transfers between devices  16.4 us
    unnamed x135, local copies, waits for them, and re-layouts  16.1 us
  transfers between devices with their start and end apart: 10, of which 4 were waited for; matrix products, arithmetic and copies ran while one was open for 36% of the time, Pallas kernels for 0%

commit v1 on v0

--- a/solution.py
+++ b/solution.py
@@ -6,6 +6,18 @@
 HD = 64
 ROT = 16
 EPS = 1e-05
+
+
+def doubled_up(x, axis, dim):
+    ways, here, step = (lax.axis_size(axis), lax.axis_index(axis), x.shape[dim])
+    line, have = (x, 1)
+    while have < ways:
+        line = jnp.concatenate(
+            [line, lax.ppermute(line, axis, [(d, (d - have) % ways) for d in range(ways)])],
+            axis=dim,
+        )
+        have = 2 * have
+    return jnp.roll(line, here * step, axis=dim)
 
 
 def exact_gelu(values):
@@ -72,7 +84,7 @@
         lax.all_gather(fc2_bias, ("fsdp", "ctx"), axis=0, tiled=True),
         lax.all_gather(ln1_gain, ("fsdp", "ctx"), axis=0, tiled=True),
         lax.all_gather(ln1_bias, ("fsdp", "ctx"), axis=0, tiled=True),
-        lax.all_gather(ln2_gain, ("fsdp", "ctx"), axis=0, tiled=True),
+        doubled_up(ln2_gain, ("fsdp", "ctx"), 0),
         lax.all_gather(ln2_bias, ("fsdp", "ctx"), axis=0, tiled=True),
     )
     qkv_full, dense_full, up_full, down_full = (gathered[0], gathered[1], gathered[2], gathered[3])

time: 641 us -> 632 us (0.986)
  blocking collectives: 169 us -> 152 us
    all_gather x1 -> x0, blocking collectives: 13.9 us -> none  [on_device(): lax.all_gather(ln2_gain, ('fsdp', 'ctx'), axis=0, tiled=True)]
    unnamed x135 -> x142, local copies, waits for them, and re-layouts: 16.1 us -> 18.4 us
  transfers between devices with their start and end apart: 10 -> 13, of which waited for: 4 -> 5; matrix products, arithmetic and copies ran while one was open for 36% -> 37% of each run, Pallas kernels for 0% -> 0%
where the time goes in v1:
time: 632 us; the launch traced here: 624 us
  waiting for transfers between devices  210 us (33%)
  blocking collectives  152 us (24%)
  matrix products  136 us (22%)
  other arithmetic  68.8 us (11%)
  local copies, waits for them, and re-layouts  35.1 us (6%)
  between operations  15.4 us (2%)
  starting transfers between devices  6.94 us (1%)
    psum x1, waiting for transfers between devices, on_device(): lax.psum((attn_part + mlp_part).astype(jnp.bfloat16), 'tp')  156 us
    reduce_scatter x2, waiting for transfers between devices, scatter(): lax.psum_scatter(array.astype(jnp.bfloat16), both, scatter_dimension=axis...  36.1 us
    psum x1, blocking collectives, on_device(): lax.psum((grad_qkv_bias, grad_up_bias, grad_shift), both)  26.9 us
    convert_element_type x1, other arithmetic, on_device(): grad_scores = (probs * (grad_probs - inner)).astype(jnp.bfloat16)  24.7 us
    all_gather x1, blocking collectives, on_device(): lax.all_gather(w_dense, ('fsdp', 'ctx'), axis=1, tiled=True)  24.2 us
    dot_general x1, matrix products, on_device(): jnp.einsum('qhd,khd->hqk', grad_attended, all_values, preferred_element_t...  22 us
    unnamed x142, local copies, waits for them, and re-layouts  18.4 us
    unnamed x12, waiting for transfers between devices  16.1 us
  transfers between devices with their start and end apart: 13, of which 5 were waited for; matrix products, arithmetic and copies ran while one was open for 37% of the time, Pallas kernels for 0%

profile of v1, /device:TPU:0, one launch (start us, length us, event | category | flops | bytes accessed | tf_op | source)
XLA Modules:
  0.0 624.4 jit_solution(5250205102601865236)
XLA Ops:
  7.3 1.9 copy.40
  10.0 3.4 collective-permute-start
  13.6 1.9 convert_reduce_fusion.1
  15.5 1.7 fusion.15
  17.3 12.0 %all-gather = bf16[8,1,128]{2,1,0:T(2,128)(2,1)S(1)} all-gather(bf16[1,1,128]{2,1,0:T(2,128)(2,1)S(1)} %bitcast.159), channel_id=1, replica_groups=mesh['fsdp'=2,'ctx'=4,'tp'=4] {'fsdp','ctx'}, dimensions={0}, use_global_device_ids=true | all-gather | bytes 2304 | tf_op jit(solution)/shard_map/all_gather | solution.py:85
  29.3 13.9 %all-gather.1 = bf16[8,1,128]{2,1,0:T(2,128)(2,1)S(1)} all-gather(bf16[1,1,128]{2,1,0:T(2,128)(2,1)S(1)} %bitcast.160), channel_id=1, replica_groups=mesh['fsdp'=2,'ctx'=4,'tp'=4] {'fsdp','ctx'}, dimensions={0}, use_global_device_ids=true | all-gather | bytes 2304 | tf_op jit(solution)/shard_map/all_gather | solution.py:86
  44.8 24.2 %all_gather.38 = bf16[256,1024]{1,0:T(8,128)(2,1)S(1)} all-gather(bf16[256,128]{1,0:T(8,128)(2,1)S(1)} %copy-done.30), channel_id=1, replica_groups=mesh['fsdp'=2,'ctx'=4,'tp'=4] {'fsdp','ctx'}, dimensions={1}, use_global_device_ids=true | all-gather | bytes 589824 | tf_op jit(solution)/shard_map/all_gather | solution.py:80
  69.9 2.6 convolution_convert_fusion.5
  72.5 3.0 fusion.2
  75.6 2.2 collective-permute-start.1
  78.4 0.9 collective-permute-done.1
  79.6 12.9 %all-gather.2 = bf16[8,1,128]{2,1,0:T(2,128)(2,1)S(1)} all-gather(bf16[1,1,128]{2,1,0:T(2,128)(2,1)S(1)} %bitcast.158), channel_id=1, replica_groups=mesh['fsdp'=2,'ctx'=4,'tp'=4] {'fsdp','ctx'}, dimensions={0}, use_global_device_ids=true | all-gather | bytes 2304 | tf_op jit(solution)/shard_map/all_gather | solution.py:88
  95.4 3.6 fusion.40
  100.3 13.1 %all_gather.37 = bf16[1024,256]{0,1:T(8,128)(2,1)S(1)} all-gather(bf16[256,256]{0,1:T(8,128)(2,1)S(1)} %bitcast.141), channel_id=1, replica_groups=mesh['fsdp'=2,'ctx'=4,'tp'=4] {'ctx'}, dimensions={0}, use_global_device_ids=true | all-gather | bytes 655360 | tf_op jit(solution)/shard_map/all_gather | solution.py:142
  113.4 12.8 %fusion = (f32[4,1024]{1,0:T(4,128)S(1)}, f32[4,1024,1792]{2,1,0:T(8,128)}) fusion(pred[1024,1792]{1,0:T(8,128)(4,1)S(1)} %fusion.2, bf16[1024,4,48]{0,2,1:T(8,128)(2,1)S(1)} %slice.242, bf16[1024,4,16]{0,2,1:T(8,128)(2,1)S(1)} %get-tuple-element.95, bf16[1024,4,64]{0,2,1:T(8,128)(2,1)S(1)} %bitcast.119, bf16[1024,4,48]{0,2,1:T(8,128)(2,1)S(1)} %slice.243, ...), kind=kOutput, calls=%fused_computation.5 | convolution fusion | flops 966717440 | bytes 32784384 | tf_op jit(solution)/shard_map/qhd,khd->hqk/dot_general | solution.py:49
  126.2 13.8 %exponential_reduce_fusion = f32[4,1024]{1,0:T(4,128)S(1)} fusion(f32[4,1024,1792]{2,1,0:T(8,128)} %get-tuple-element.107, f32[4,1024]{1,0:T(4,128)S(1)} %get-tuple-element.106, pred[1024,1792]{1,0:T(8,128)(4,1)S(1)} %fusion.2), kind=kLoop, calls=%fused_computation.3 | loop fusion | flops 29356032 | bytes 31227904 | tf_op jit(solution)/shard_map/reduce_sum | solution.py:155
  140.1 12.0 %all_gather.36 = bf16[1024,256]{0,1:T(8,128)(2,1)S(1)} all-gather(bf16[256,256]{0,1:T(8,128)(2,1)S(1)} %bitcast.142), channel_id=1, replica_groups=mesh['fsdp'=2,'ctx'=4,'tp'=4] {'ctx'}, dimensions={0}, use_global_device_ids=true | all-gather | bytes 655360 | tf_op jit(solution)/shard_map/all_gather | solution.py:143
  152.1 22.0 %multiply_reduce_fusion = (f32[4,1024]{1,0:T(4,128)S(1)}, f32[4,1024,1792]{2,1,0:T(8,128)}) fusion(f32[4,1024,1792]{2,1,0:T(8,128)} %get-tuple-element.107, f32[4,1024]{1,0:T(4,128)S(1)} %log_add_fusion, pred[1024,1792]{1,0:T(8,128)(4,1)S(1)} %fusion.2, bf16[1024,4,64]{0,2,1:T(8,128)(2,1)S(1)} %bitcast.133, bf16[768,4,64]{0,2,1:T(8,128)(2,1)S(1)} %slice_bitcast_fusion.4, ...), kind=kOutput, calls=%fused_computation.1 | convolution fusion | flops 978055168 | bytes 62029824 | tf_op jit(solution)/shard_map/qhd,khd->hqk/dot_general | solution.py:183
  174.1 24.7 %multiply_convert_fusion = bf16[4,1024,1792]{2,1,0:T(8,128)(2,1)} fusion(f32[4,1024,1792]{2,1,0:T(8,128)} %get-tuple-element.109, f32[4,1024,1792]{2,1,0:T(8,128)} %get-tuple-element.107, f32[4,1024]{1,0:T(4,128)S(1)} %get-tuple-element.108, f32[4,1024]{1,0:T(4,128)S(1)} %log_add_fusion, pred[1024,1792]{1,0:T(8,128)(4,1)S(1)} %fusion.2), kind=kLoop, calls=%fused_computation | loop fusion | flops 44040192 | bytes 75268096 | tf_op jit(solution)/shard_map/convert_element_type | solution.py:187
  198.7 7.8 %fusion.25 = f32[1792,4,64]{0,2,1:T(8,128)S(1)} fusion(bf16[4,1024,1792]{2,1,0:T(8,128)(2,1)} %multiply_convert_fusion, bf16[1024,4,48]{0,2,1:T(8,128)(2,1)S(1)} %slice.243, bf16[1024,4,16]{0,2,1:T(8,128)(2,1)S(1)} %get-tuple-element.96), kind=kOutput, calls=%fused_computation.57 | convolution fusion | flops 941031424 | bytes 17039360 | tf_op jit(solution)/shard_map/hqk,qhd->khd/dot_general | solution.py:193
  206.5 0.9 slice.241
  207.4 0.9 slice.176
  208.4 14.1 %convolution_convert_fusion.3 = bf16[4,64,1024]{2,1,0:T(8,128)(2,1)} fusion(bf16[768,4,64]{0,2,1:T(8,128)(2,1)} %copy-done.13, bf16[1024,4,64]{0,2,1:T(8,128)(2,1)} %bitcast.118, f32[4,1024,1792]{2,1,0:T(8,128)} %get-tuple-element.107, f32[4,1024]{1,0:T(4,128)S(1)} %log_add_fusion, pred[1024,1792]{1,0:T(8,128)(4,1)S(1)} %fusion.2), kind=kOutput, calls=%fused_computation.83 | convolution fusion | flops 970981376 | bytes 32653312 | tf_op jit(solution)/shard_map/hqk,khd->qhd/dot_general | solution.py:157
  223.0 13.7 %convolution_bitcast_fusion = bf16[1792,4,64]{0,2,1:T(8,128)(2,1)S(1)} fusion(bf16[1024,4,64]{0,2,1:T(8,128)(2,1)} %bitcast.132, f32[4,1024,1792]{2,1,0:T(8,128)} %get-tuple-element.107, f32[4,1024]{1,0:T(4,128)S(1)} %log_add_fusion, pred[1024,1792]{1,0:T(8,128)(4,1)S(1)} %fusion.2), kind=kOutput, calls=%fused_computation.56 | convolution fusion | flops 968884224 | bytes 32653312 | tf_op jit(solution)/shard_map/hqk,qhd->khd/dot_general | solution.py:195
  236.6 0.9 slice.240
  238.4 10.2 %fusion.43 = f32[1024,4,64]{0,2,1:T(8,128)S(1)} fusion(bf16[4,1024,1792]{2,1,0:T(8,128)(2,1)} %multiply_convert_fusion, bf16[1024,4,48]{0,2,1:T(8,128)(2,1)} %copy-done.6, bf16[1024,4,16]{0,2,1:T(8,128)(2,1)S(1)} %get-tuple-element.95, bf16[1024,4,64]{0,2,1:T(8,128)(2,1)} %bitcast.120), kind=kOutput, calls=%fused_computation.82 | convolution fusion | flops 943915008 | bytes 16777216 | tf_op jit(solution)/shard_map/hqk,khd->qhd/dot_general | solution.py:189
  248.6 1.0 copy-done.5
  250.4 1.5 convolution_convert_fusion.4
  251.9 2.1 copy.45
  254.0 1.6 slice_negate_fusion
  255.8 15.9 %multiply_convert_fusion.1 = (bf16[1024,1024]{1,0:T(8,128)(2,1)S(1)}, f32[1024,1024]{1,0:T(8,128)}, f32[1024,1024]{1,0:T(8,128)}) fusion(f32[1024]{0:T(1024)S(1)} %copy-done.39, bf16[1024,1024]{1,0:T(8,128)(2,1)} %all-gather.11.cloned.1.call-done, f32[1024]{0:T(1024)S(1)} %bitcast.151, f32[1024]{0:T(1024)S(1)} %copy-done.43, f32[1024]{0:T(1024)S(1)} %copy-done.34, ...), kind=kOutput, calls=%fused_computation.39 | convolution fusion | flops 2226126848 | bytes 14700544 | tf_op jit(solution)/shard_map/dot_general | solution.py:160
  271.7 1.3 copy-done.60
  273.0 3.8 convolution_convert_fusion
  276.8 3.9 copy.47
  281.0 4.7 fusion.80
  285.8 2.1 add_convert_fusion.2
  287.9 0.9 copy-done.57
  288.8 5.2 convert_reduce_fusion.3
  294.0 1.0 convert.34
  295.1 1.0 fusion.59
  296.3 1.2 maximum_bitcast_fusion.1
  297.9 1.9 fusion.81
  300.6 3.8 add_convert_fusion
  304.5 5.8 convolution_convert_fusion.1
  310.5 12.3 %all-gather.3 = bf16[8,1,128]{2,1,0:T(2,128)(2,1)S(1)} all-gather(bf16[1,1,128]{2,1,0:T(2,128)(2,1)S(1)} %bitcast.161), channel_id=1, replica_groups=mesh['fsdp'=2,'ctx'=4,'tp'=4] {'fsdp','ctx'}, dimensions={0}, use_global_device_ids=true | all-gather | bytes 2304 | tf_op jit(solution)/shard_map/all_gather | solution.py:83
  322.8 13.4 %all-gather.4 = bf16[8,1,128]{2,1,0:T(2,128)(2,1)S(1)} all-gather(bf16[1,1,128]{2,1,0:T(2,128)(2,1)S(1)} %bitcast.162), channel_id=1, replica_groups=mesh['fsdp'=2,'ctx'=4,'tp'=4] {'fsdp','ctx'}, dimensions={0}, use_global_device_ids=true | all-gather | bytes 2304 | tf_op jit(solution)/shard_map/all_gather | solution.py:84
  336.4 0.9 copy.46
  338.1 4.8 convolution_convert_fusion.2
  342.9 15.2 %reduce-scatter.21.cloned.1.call-done = bf16[128,1024]{1,0:T(8,128)(2,1)} async-done(((bf16[1024,1024]{1,0:T(8,128)(2,1)}), bf16[128,1024]{1,0:T(8,128)(2,1)}) %reduce-scatter.21.cloned.1.call-update) | async-done | bytes 262160
  358.1 1.1 copy.48
  360.1 156.4 %all-reduce.8.cloned.1.call-done = (bf16[1024,1024]{1,0:T(8,128)(2,1)}, bf16[1024,1024]{1,0:T(8,128)(2,1)}) async-done(((bf16[1024,1024]{1,0:T(8,128)(2,1)}, bf16[1024,1024]{1,0:T(8,128)(2,1)}), (bf16[1024,1024]{1,0:T(8,128)(2,1)}, bf16[1024,1024]{1,0:T(8,128)(2,1)})) %all-reduce.8.cloned.1.call-update) | async-done | bytes 4194320 | tf_op jit(solution)/shard_map/psum | solution.py:165
  516.5 3.7 convert_reduce_fusion
  520.3 6.2 convert_reduce_fusion.2
  526.4 26.9 %all-reduce.4 = (f32[768]{0:T(1024)S(1)}, f32[1024]{0:T(1024)S(1)}, f32[1024]{0:T(1024)S(1)}) all-reduce(f32[768]{0:T(1024)S(1)} %reduce_sum.126, f32[1024]{0:T(1024)S(1)} %get-tuple-element.79, f32[1024]{0:T(1024)S(1)} %get-tuple-element.110), channel_id=1, replica_groups=mesh['fsdp'=2,'ctx'=4,'tp'=4] {'fsdp','ctx'}, use_global_device_ids=true, to_apply=%region_13.14 | all-reduce | flops 2816 | bytes 22528 | tf_op jit(solution)/shard_map/psum | solution.py:257
  553.3 4.3 slice.170
  557.6 1.9 slice.186
  559.7 1.0 reduce-scatter.17.cloned.1.call-done
  560.7 2.0 fusion.51
  562.7 2.3 slice_bitcast_fusion
  565.0 2.3 slice_bitcast_fusion.1
  567.3 35.0 %reduce-scatter.15.cloned.1.call-done = bf16[128,768]{1,0:T(8,128)(2,1)} async-done(((bf16[1024,768]{1,0:T(8,128)(2,1)}), bf16[128,768]{1,0:T(8,128)(2,1)}) %reduce-scatter.15.cloned.1.call-update) | async-done | bytes 196624 | tf_op jit(solution)/shard_map/reduce_scatter | solution.py:249
  602.3 1.1 fusion.54
  603.4 11.7 %psum.47 = f32[4,128]{1,0:T(4,128)S(1)} all-reduce(f32[4,128]{1,0:T(4,128)S(1)} %pad_maximum_fusion.11), channel_id=1, replica_groups=mesh['fsdp'=2,'ctx'=4,'tp'=4] {'tp'}, use_global_device_ids=true, to_apply=%region_25.26 | all-reduce | flops 512 | bytes 4096 | tf_op jit(solution)/shard_map/psum | solution.py:265
  615.8 0.9 copy.44
  (227 shorter events, 15.8 us)
Async XLA Ops:
  7.2 8.3 %copy-start = (bf16[1,3,256,1024]{3,2,1,0:T(8,128)(2,1)S(1)}, bf16[1,3,256,1024]{3,2,1,0:T(8,128)(2,1)}, u32[]{:S(2)}) copy-start(bf16[1,3,256,1024]{3,2,1,0:T(8,128)(2,1)} %param.18) | copy-start | bytes 4718596
  7.2 10.1 %copy-start.50 = (bf16[128]{0:T(256)(128)(2,1)S(1)}, bf16[128]{0:T(256)(128)(2,1)}, u32[]{:S(2)}) copy-start(bf16[128]{0:T(256)(128)(2,1)} %param.28) | copy-start | bytes 772
  7.2 22.1 %copy-start.52 = (bf16[128]{0:T(256)(128)(2,1)S(1)}, bf16[128]{0:T(256)(128)(2,1)}, u32[]{:S(2)}) copy-start(bf16[128]{0:T(256)(128)(2,1)} %param.29) | copy-start | bytes 772
  7.2 36.0 %copy-start.47 = (s32[1,3]{1,0:T(1,128)S(1)}, s32[1,3]{1,0:T(1,128)}, u32[]{:S(2)}) copy-start(s32[1,3]{1,0:T(1,128)} %param.19) | copy-start | bytes 40
  7.2 37.6 %copy-start.30 = (bf16[256,128]{1,0:T(8,128)(2,1)S(1)}, bf16[256,128]{1,0:T(8,128)(2,1)}, u32[]{:S(2)}) copy-start(bf16[256,128]{1,0:T(8,128)(2,1)} %param.22) | copy-start | bytes 196612
  7.2 62.7 %copy-start.14 = (bf16[1,3,256,1024]{3,2,1,0:T(8,128)(2,1)S(1)}, bf16[1,3,256,1024]{3,2,1,0:T(8,128)(2,1)}, u32[]{:S(2)}) copy-start(bf16[1,3,256,1024]{3,2,1,0:T(8,128)(2,1)} %param.33) | copy-start | bytes 4718596
  7.2 88.2 %all-gather.9.cloned.1.call-start = ((), (), s32[]{:S(2)}) async-start(), calls=%async_computation.6 | async-start | bytes 1769472 | tf_op jit(solution)/shard_map/all_gather | solution.py:79
  9.2 246.5 %all-gather.11.cloned.1.call-start = ((), (), s32[]{:S(2)}) async-start(), calls=%async_computation.7 | async-start | bytes 2359296 | tf_op jit(solution)/shard_map/all_gather | solution.py:81
  10.0 271.0 %all-gather.13.cloned.1.call-start = ((), (), s32[]{:S(2)}) async-start(), calls=%async_computation.8 | async-start | bytes 2359296 | tf_op jit(solution)/shard_map/all_gather | solution.py:82
  10.0 65.5 %collective-permute-start = (bf16[128]{0:T(256)(128)(2,1)}, bf16[128]{0:T(256)(128)(2,1)S(1)}, u32[]{:S(2)}, u32[]{:S(2)}) collective-permute-start(bf16[128]{0:T(256)(128)(2,1)} %param.30), channel_id=1, source_target_pairs={{0,28},{4,0},{8,4},{12,8},{16,12},{20,16},{24,20},{28,24},{1,29},{... | collective-permute-start | bytes 776 | tf_op jit(solution)/shard_map/ppermute | solution.py:16
  13.5 280.6 %reduce-scatter.11.cloned.1.call-start = ((), (), s32[]{:S(2)}) async-start(), calls=%async_computation.9 | async-start | bytes 655360 | tf_op jit(solution)/shard_map/reduce_scatter | solution.py:199
  15.5 79.9 %copy-start.31 = (f32[1024]{0:T(1024)}, f32[1024]{0:T(1024)S(1)}, u32[]{:S(2)}) copy-start(f32[1024]{0:T(1024)S(1)} %broadcast_multiply_fusion.2) | copy-start | bytes 12292
  17.3 78.2 %copy-start.33 = (f32[1024]{0:T(1024)}, f32[1024]{0:T(1024)S(1)}, u32[]{:S(2)}) copy-start(f32[1024]{0:T(1024)S(1)} %add_rsqrt_fusion) | copy-start | bytes 12292
  43.3 32.2 %copy-start.45 = (bf16[3,256]{1,0:T(4,128)(2,1)S(1)}, bf16[3,256]{1,0:T(4,128)(2,1)}, u32[]{:S(2)}) copy-start(bf16[3,256]{1,0:T(4,128)(2,1)} %param.21) | copy-start | bytes 4612
  43.3 32.3 %copy-start.36 = (bf16[128]{0:T(256)(128)(2,1)S(1)}, bf16[128]{0:T(256)(128)(2,1)}, u32[]{:S(2)}) copy-start(bf16[128]{0:T(256)(128)(2,1)} %param.30) | copy-start | bytes 772
  43.5 34.3 %copy-start.46 = (bf16[1024]{0:T(1024)(128)(2,1)S(1)}, bf16[1024]{0:T(1024)(128)(2,1)}, u32[]{:S(2)}) copy-start(bf16[1024]{0:T(1024)(128)(2,1)} %param.25) | copy-start | bytes 6148
  43.5 36.1 %copy-start.48 = (bf16[128]{0:T(256)(128)(2,1)S(1)}, bf16[128]{0:T(256)(128)(2,1)}, u32[]{:S(2)}) copy-start(bf16[128]{0:T(256)(128)(2,1)} %param.31) | copy-start | bytes 772
  75.5 23.5 %copy-start.40 = (f32[8,1,128]{2,1,0:T(1,128)}, f32[8,1,128]{2,1,0:T(1,128)S(1)}, u32[]{:S(2)}) copy-start(f32[8,1,128]{2,1,0:T(1,128)S(1)} %convert_element_type.249) | copy-start | bytes 12292
  75.6 3.7 collective-permute-start.1
  79.3 14.5 %collective-permute-start.2 = (bf16[512]{0:T(512)(128)(2,1)S(1)}, bf16[512]{0:T(512)(128)(2,1)S(1)}, u32[]{:S(2)}, u32[]{:S(2)}) collective-permute-start(bf16[512]{0:T(512)(128)(2,1)S(1)} %pad_maximum_fusion.12), channel_id=1, source_target_pairs={{0,16},{4,20},{8,24},{12,28},{16,0},{20,4},{24,8},{28,12},{1,17},{... | collective-permute-start | bytes 3080 | tf_op jit(solution)/shard_map/ppermute | solution.py:16
  99.4 14.1 %copy-start.6 = (bf16[1024,4,48]{0,2,1:T(8,128)(2,1)}, bf16[1024,4,48]{0,2,1:T(8,128)(2,1)S(1)}, u32[]{:S(2)}) copy-start(bf16[1024,4,48]{0,2,1:T(8,128)(2,1)S(1)} %slice.242) | copy-start | bytes 1179652
  99.8 52.3 %copy-start.13 = (bf16[768,4,64]{0,2,1:T(8,128)(2,1)}, bf16[768,4,64]{0,2,1:T(8,128)(2,1)S(1)}, u32[]{:S(2)}) copy-start(bf16[768,4,64]{0,2,1:T(8,128)(2,1)S(1)} %slice_bitcast_fusion.4) | copy-start | bytes 1179652
  113.4 12.8 %copy-start.12 = (bf16[1024,256]{0,1:T(8,128)(2,1)}, bf16[1024,256]{0,1:T(8,128)(2,1)S(1)}, u32[]{:S(2)}) copy-start(bf16[1024,256]{0,1:T(8,128)(2,1)S(1)} %all_gather.37) | copy-start | bytes 1572868
  126.2 25.8 %copy-start.23 = (bf16[1024,256]{0,1:T(8,128)(2,1)S(1)}, bf16[1024,256]{0,1:T(8,128)(2,1)}, u32[]{:S(2)}) copy-start(bf16[1024,256]{0,1:T(8,128)(2,1)} %convolution_convert_fusion.5) | copy-start | bytes 1572868
  152.0 22.0 %copy-start.8 = (bf16[1024,256]{0,1:T(8,128)(2,1)}, bf16[1024,256]{0,1:T(8,128)(2,1)S(1)}, u32[]{:S(2)}) copy-start(bf16[1024,256]{0,1:T(8,128)(2,1)S(1)} %all_gather.36) | copy-start | bytes 1572868
  222.5 73.7 %reduce-scatter.13.cloned.1.call-start = ((), (), s32[]{:S(2)}) async-start(), calls=%async_computation.10 | async-start | bytes 655360 | tf_op jit(solution)/shard_map/reduce_scatter | solution.py:205
  238.3 12.1 %copy-start.24 = (bf16[4,64,1024]{2,1,0:T(8,128)(2,1)S(1)}, bf16[4,64,1024]{2,1,0:T(8,128)(2,1)}, u32[]{:S(2)}) copy-start(bf16[4,64,1024]{2,1,0:T(8,128)(2,1)} %convolution_convert_fusion.3) | copy-start | bytes 1572868
  238.3 12.1 %copy-start.25 = (bf16[1,256,1024]{2,1,0:T(8,128)(2,1)S(1)}, bf16[1,256,1024]{2,1,0:T(8,128)(2,1)}, u32[]{:S(2)}) copy-start(bf16[1,256,1024]{2,1,0:T(8,128)(2,1)} %param.32) | copy-start | bytes 1572868
  238.3 98.0 %reduce-scatter.19.cloned.1.call-start = ((), (), s32[]{:S(2)}) async-start(), calls=%async_computation.13 | async-start | bytes 589824
  238.4 12.0 %copy-start.15 = (bf16[1,3,256,1024]{3,2,1,0:T(8,128)(2,1)S(1)}, bf16[1,3,256,1024]{3,2,1,0:T(8,128)(2,1)}, u32[]{:S(2)}) copy-start(bf16[1,3,256,1024]{3,2,1,0:T(8,128)(2,1)} %param.33) | copy-start | bytes 4718596
  249.6 6.1 copy-start.4
  249.6 6.2 copy-start.32
  249.6 6.2 copy-start.34
  249.6 6.2 copy-start.39
  249.6 6.2 copy-start.42
  249.6 6.2 copy-start.43
  255.6 102.5 %reduce-scatter.21.cloned.1.call-start = ((), (), s32[]{:S(2)}) async-start(), calls=%async_computation.14 | async-start | bytes 2359296
  255.8 17.2 %copy-start.16 = (bf16[1,3,256,1024]{3,2,1,0:T(8,128)(2,1)S(1)}, bf16[1,3,256,1024]{3,2,1,0:T(8,128)(2,1)}, u32[]{:S(2)}) copy-start(bf16[1,3,256,1024]{3,2,1,0:T(8,128)(2,1)} %param.33) | copy-start | bytes 4718596
  280.8 5.0 copy-start.10
  280.8 235.7 %all-reduce.8.cloned.1.call-start = ((), (), s32[]{:S(2)}) async-start(), calls=%async_computation.15 | async-start | bytes 8388608 | tf_op jit(solution)/shard_map/psum | solution.py:165
  281.0 6.8 %copy-start.61 = (f32[1024,1024]{1,0:T(8,128)S(1)}, f32[1024,1024]{1,0:T(8,128)}, u32[]{:S(2)}) copy-start(f32[1024,1024]{1,0:T(8,128)} %get-tuple-element.76) | copy-start | bytes 12582916
  281.0 6.8 %copy-start.62 = (f32[1024,1024]{1,0:T(8,128)S(1)}, f32[1024,1024]{1,0:T(8,128)}, u32[]{:S(2)}) copy-start(f32[1024,1024]{1,0:T(8,128)} %get-tuple-element.105) | copy-start | bytes 12582916
  285.8 3.0 copy-start.57
  288.8 6.2 copy-start.2
  288.8 6.3 %copy-start.22 = (f32[1024,16]{0,1:T(8,128)S(1)}, f32[1024,16]{0,1:T(8,128)}, u32[]{:S(2)}) copy-start(f32[1024,16]{0,1:T(8,128)} %pad_maximum_fusion.9) | copy-start | bytes 196612
  288.8 6.3 %copy-start.27 = (f32[1024,4,8]{0,2,1:T(8,128)S(1)}, f32[1024,4,8]{0,2,1:T(8,128)}, u32[]{:S(2)}) copy-start(f32[1024,4,8]{0,2,1:T(8,128)} %get-tuple-element.83) | copy-start | bytes 393220
  288.8 6.3 %copy-start.28 = (f32[1024,16]{0,1:T(8,128)S(1)}, f32[1024,16]{0,1:T(8,128)}, u32[]{:S(2)}) copy-start(f32[1024,16]{0,1:T(8,128)} %get-tuple-element.97) | copy-start | bytes 196612
  294.0 2.2 copy-start.18
  297.9 2.8 copy-start.63
  304.4 6.0 copy-start.37
  304.4 6.0 copy-start.49
  304.4 6.0 copy-start.51
  304.4 6.0 copy-start.53
  304.4 6.0 copy-start.54
  304.5 18.3 %copy-start.55 = (bf16[128]{0:T(256)(128)(2,1)S(1)}, bf16[128]{0:T(256)(128)(2,1)}, u32[]{:S(2)}) copy-start(bf16[128]{0:T(256)(128)(2,1)} %param.27) | copy-start | bytes 772
  304.5 31.7 %copy-start.7 = (bf16[128,3,256]{0,2,1:T(8,128)(2,1)S(1)}, bf16[128,3,256]{0,2,1:T(8,128)(2,1)}, u32[]{:S(2)}) copy-start(bf16[128,3,256]{0,2,1:T(8,128)(2,1)} %copy.40) | copy-start | bytes 589828
  304.5 256.2 %reduce-scatter.17.cloned.1.call-start = ((), (), s32[]{:S(2)}) async-start(), calls=%async_computation.12 | async-start | bytes 2359296 | tf_op jit(solution)/shard_map/reduce_scatter | solution.py:249
  310.4 292.0 %reduce-scatter.15.cloned.1.call-start = ((), (), s32[]{:S(2)}) async-start(), calls=%async_computation.11 | async-start | bytes 1769472 | tf_op jit(solution)/shard_map/reduce_scatter | solution.py:249
  516.5 3.7 copy-start.3
  516.5 3.8 copy-start.11
  553.3 7.4 %copy-start.38 = (f32[1024]{0:T(1024)}, f32[1024]{0:T(1024)S(1)}, u32[]{:S(2)}) copy-start(f32[1024]{0:T(1024)S(1)} %get-tuple-element.141) | copy-start | bytes 12292
  553.3 6.2 copy-start.35
  553.3 4.3 copy-start.1
  557.6 3.1 copy-start.20
  (13 other events, 19.1 us)
Sparse Core Ops, SparseCore 0:
  10.0 28.5 all-gather.8
  40.5 33.1 all-gather.10
  75.6 27.6 all-gather.12
  222.6 25.1 reduce-scatter.10
  251.4 24.7 reduce-scatter.12
  279.1 34.1 reduce-scatter.18
  316.9 41.2 reduce-scatter.20
  361.1 155.3 all-reduce.7
  520.1 40.5 reduce-scatter.16
  563.9 38.4 reduce-scatter.14
